TPU v7x, 32 devices: a whole 2x2x4 slice. The times are simulated.
32 devices in a mesh: particle: 2 (over x), coil: 8 (over z, y), phase: 2 (over core).
Axes of the slice: x: 2, y: 2, z: 4, core: 2. Of those that a mesh axis runs over, the one named last changes fastest.
Arguments:
- position: float32 [256, 16, 4, 384], P('coil', 'phase', 'particle'), parts along dimension 2, may hold values from -6 to 6
- coil_maps: bfloat16 [8, 256, 4, 384], P('coil', None, 'particle'), parts along dimension 2, may hold values from -2 to 2
- kspace_data: bfloat16 [8, 256, 16, 4, 384], P('coil', None, 'phase', 'particle'), parts along dimension 3, may hold values from -1.796875 to 1.796875
- sample_mask: int32 [256, 16], P(None, 'phase'), may hold values 0 or 1
Outputs:
- gradient: float32 [256, 16, 4, 384], P('coil', 'phase', 'particle'), parts along dimension 2
There are 2 independent parts, one for each index of `particle`. A program takes and returns all parts, laid end to end along the dimension named above; an argument that names none is the same for every part. Nothing has to cross between parts.
All inputs are finite; a program needn't handle non-finite values. No bound on the sum of `sample_mask` on one device may be relied on, other than what follows from the above.
Results may differ from a plain program's by a relative error of at most 0.0012.
Values may be sent and summed in bfloat16 or wider, within the bound.
A program may use at most 64 MiB of HBM per device.

v0:
```python
import math
import jax
import jax.numpy as jnp
from jax import lax
from jax.sharding import PartitionSpec as P


def with_halo(block, sides, width):
    for axis, dim in sides:
        count = lax.axis_size(axis)
        forward = [(i, i + 1) for i in range(count - 1)]
        forward.append((count - 1, 0))
        backward = [(target, source) for source, target in forward]
        low = lax.ppermute(
            lax.slice_in_dim(block, block.shape[dim] - width, None, axis=dim), axis, forward
        )
        high = lax.ppermute(lax.slice_in_dim(block, 0, width, axis=dim), axis, backward)
        block = jnp.concatenate([low, block, high], axis=dim)
    return block


def dft_tables(length):
    counter = jnp.arange(length, dtype=jnp.int32)
    product = counter[:, None] * counter[None, :] % length
    angles = product.astype(jnp.float32) * (2.0 * math.pi / length)
    scaling = 1.0 / math.sqrt(length)
    return (jnp.cos(angles) * scaling, -jnp.sin(angles) * scaling)


def build_tables(rows_total, width):
    row_real, row_imag = dft_tables(rows_total)
    col_real, col_imag = dft_tables(width)
    forward_wide = jnp.concatenate(
        [jnp.concatenate([col_real, col_imag], 1), jnp.concatenate([-col_imag, col_real], 1)], 0
    )
    backward_wide = jnp.concatenate(
        [jnp.concatenate([col_real, -col_imag], 1), jnp.concatenate([col_imag, col_real], 1)], 0
    )
    return (
        row_real.astype(jnp.bfloat16),
        row_imag.astype(jnp.bfloat16),
        forward_wide.astype(jnp.bfloat16),
        backward_wide.astype(jnp.bfloat16),
    )


def complex_times(factor, values, conjugate):
    width = values.shape[-1] // 2
    factor_real = factor[..., :width]
    factor_imag = factor[..., width:]
    if conjugate:
        factor_imag = -factor_imag
    value_real = values[..., :width]
    value_imag = values[..., width:]
    out_real = factor_real * value_real - factor_imag * value_imag
    out_imag = factor_real * value_imag + factor_imag * value_real
    return jnp.concatenate([out_real, out_imag], -1)


def rows_apply(table_real, table_imag, values, adjoint):
    width = values.shape[-1] // 2
    real_part = jnp.einsum("kn,npsd->kpsd", table_real, values, preferred_element_type=jnp.float32)
    imag_part = jnp.einsum("kn,npsd->kpsd", table_imag, values, preferred_element_type=jnp.float32)
    if adjoint:
        out_real = real_part[..., :width] + imag_part[..., width:]
        out_imag = real_part[..., width:] - imag_part[..., :width]
    else:
        out_real = real_part[..., :width] - imag_part[..., width:]
        out_imag = real_part[..., width:] + imag_part[..., :width]
    return jnp.concatenate([out_real, out_imag], -1)


def local(position, coil_maps, kspace_data, sample_mask):
    rows_here = position.shape[0]
    rows_total = coil_maps.shape[1]
    width = position.shape[3] // 2
    row_real, row_imag, forward_wide, backward_wide = build_tables(rows_total, width)
    coil_map = coil_maps[0]
    coil_data = kspace_data[0]
    sample_weight = sample_mask.astype(jnp.float32)[:, :, None, None]
    position_low = position.astype(jnp.bfloat16)
    map_rows = coil_map.astype(jnp.float32)[:, None]
    lifted = complex_times(
        map_rows,
        lax.all_gather(position_low, "coil", axis=0, tiled=True).astype(jnp.float32),
        False,
    ).astype(jnp.bfloat16)
    spread = jnp.einsum(
        "npsc,cd->npsd", lifted, forward_wide, preferred_element_type=jnp.float32
    ).astype(jnp.bfloat16)
    kspace = rows_apply(row_real, row_imag, spread, False)
    residual = (sample_weight * (kspace - coil_data.astype(jnp.float32))).astype(jnp.bfloat16)
    back_rows = rows_apply(row_real, row_imag, residual, True).astype(jnp.bfloat16)
    back = jnp.einsum("npsc,cd->npsd", back_rows, backward_wide, preferred_element_type=jnp.float32)
    map_rows = coil_map.astype(jnp.float32)[:, None]
    summed = lax.psum(complex_times(map_rows, back, True), "coil")
    likelihood = lax.dynamic_slice_in_dim(summed, lax.axis_index("coil") * rows_here, rows_here, 0)
    padded = with_halo(position, (("coil", 0), ("phase", 1)), 1)
    phase_part = 2.0 * position - padded[1:-1, :-2] - padded[1:-1, 2:]
    row_part = 2.0 * position - padded[:-2, 1:-1] - padded[2:, 1:-1]
    return 0.6 * likelihood + 0.5 * phase_part + 0.3 * row_part


def solution(mesh):
    in_specs = (
        P("coil", "phase", "particle", None),
        P("coil", None, "particle", None),
        P("coil", None, "phase", "particle", None),
        P(None, "phase"),
    )
    out_specs = P("coil", "phase", "particle", None)
    return jax.shard_map(local, mesh=mesh, in_specs=in_specs, out_specs=out_specs, check_vma=False)
```

profile of v0, /device:TPU:0, one launch (start us, length us, event | category | flops | bytes accessed | tf_op | source)
XLA Modules:
  0.0 333.7 jit_solution(8550984614529454720)
XLA Ops:
  6.5 0.0 copy-start.4
  6.5 0.0 all-gather.2.cloned.1.call-start
  6.5 2.1 copy.23
  8.7 0.0 all-gather.2.cloned.1.call-update
  8.7 0.0 all-reduce.2.cloned.1.call-start
  8.8 1.3 bitcast_convert_fusion
  10.0 0.7 negate_bitcast_fusion
  10.8 0.0 copy-start
  10.9 0.0 copy-done.4
  10.9 0.9 copy.9
  11.8 0.8 fusion.44
  12.6 0.8 negate_convert_fusion
  13.4 58.9 %all-gather.2.cloned.1.call-done = bf16[256,8,2,384]{3,0,2,1:T(8,128)(2,1)} async-done(((bf16[32,8,2,384]{3,0,2,1:T(8,128)(2,1)}), bf16[256,8,2,384]{3,0,2,1:T(8,128)(2,1)}) %all-gather.2.cloned.1.call-update) | async-done | bytes 3145744 | tf_op jit(solution)/shard_map/all_gather | solution.py:85
  72.3 2.5 convert_element_type.81
  74.9 0.0 copy-done
  74.9 1.8 subtract_convert_fusion
  76.7 2.3 fusion.12
  79.0 1.9 fusion.49
  80.9 4.6 %fusion.53 = f32[256,8,2,384]{3,0,2,1:T(8,128)} fusion(bf16[256,8,2,384]{3,0,2,1:T(8,128)(2,1)S(1)} %fusion.12), kind=kOutput, calls=%fused_computation.82 | convolution fusion | flops 806354944 | bytes 9437184 | tf_op jit(solution)/shard_map/kn,npsd->kpsd/dot_general | solution.py:62
  85.4 9.2 %slice_subtract_fusion.1 = (f32[256,8,2,192]{3,0,2,1:T(8,128)}, f32[256,8,2,192]{3,0,2,1:T(8,128)}) fusion(f32[256,8,2,384]{3,0,2,1:T(8,128)S(1)} %fusion.49, f32[256,8,2,384]{3,0,2,1:T(8,128)} %fusion.53), kind=kLoop, calls=%fused_computation.9 | loop fusion | flops 1572864 | bytes 18874368 | tf_op jit(solution)/shard_map/sub | solution.py:68
  94.7 5.3 %fusion.1 = bf16[256,8,2,384]{3,0,2,1:T(8,128)(2,1)S(1)} fusion(f32[256,8,2,192]{3,0,2,1:T(8,128)} %get-tuple-element.8, f32[256,8,2,192]{3,0,2,1:T(8,128)} %get-tuple-element.7, bf16[1,256,8,2,384]{4,3,2,1,0:T(2,128)(2,1)} %param.6, f32[256,8]{0,1:T(8,128)S(1)} %convert_element_type.79), kind=kLoop, calls=%fused_computation.2 | loop fusion | flops 7864320 | bytes 12591104 | tf_op jit(solution)/shard_map/convert_element_type | solution.py:92
  100.0 1.9 fusion.47
  101.9 1.9 fusion.51
  103.8 2.6 fusion.3
  106.4 0.0 copy-start.1
  106.4 0.0 copy-start.3
  106.4 2.3 fusion.8
  108.7 0.0 copy-done.1
  108.7 0.0 copy-done.3
  108.7 2.0 multiply_subtract_fusion
  110.8 3.9 %pad_maximum_fusion = f32[256,8,2,384]{3,0,2,1:T(8,128)} fusion(f32[256,8,2,192]{3,0,2,1:T(8,128)S(1)} %get-tuple-element.10, f32[256,8,2,192]{3,0,2,1:T(8,128)S(1)} %get-tuple-element.9), kind=kLoop, calls=%fused_computation.3 | loop fusion | flops 1572864 | bytes 12582912 | tf_op jit(solution)/shard_map/concatenate | solution.py:57
  114.7 0.0 copy-start.2
  114.7 0.0 all-reduce.2.cloned.1.call-update
  114.7 1.1 copy-done.2
  115.9 0.6 collective-permute-start
  116.5 4.2 %collective-permute-start.1 = (f32[1,8,2,384]{3,0,2,1:T(1,128)S(1)}, f32[1,8,2,384]{3,0,2,1:T(1,128)S(1)}, u32[]{:S(2)}, u32[]{:S(2)}) collective-permute-start(f32[1,8,2,384]{3,0,2,1:T(1,128)S(1)} %copy.12), channel_id=1, source_target_pairs={{2,0},{4,2},{6,4},{8,6},{10,8},{12,10},{14,12},{0,14},{3,1},{5,3},... | collective-permute-start | bytes 73736 | tf_op jit(solution)/shard_map/ppermute | solution.py:17
  120.7 0.3 copy.6
  121.0 1.6 collective-permute-done
  122.5 0.2 collective-permute-done.1
  122.8 0.1 collective-permute-start.2
  122.8 0.5 collective-permute-start.3
  123.3 0.8 collective-permute-done.2
  124.2 0.2 collective-permute-done.3
  124.3 199.5 %all-reduce.2.cloned.1.call-done = f32[256,8,2,384]{3,0,2,1:T(8,128)} async-done(((f32[256,8,2,384]{3,0,2,1:T(8,128)}), f32[256,8,2,384]{3,0,2,1:T(8,128)}) %all-reduce.2.cloned.1.call-update) | async-done | bytes 6291472 | tf_op jit(solution)/shard_map/psum | solution.py:96
  323.8 1.6 fusion.17
  325.4 1.5 copy.16
  (7 shorter events, 0.2 us)
Async XLA Ops:
  6.5 4.3 %copy-start.4 = (s32[256,8]{0,1:T(8,128)S(1)}, s32[256,8]{0,1:T(8,128)}, u32[]{:S(2)}) copy-start(s32[256,8]{0,1:T(8,128)} %param.7) | copy-start | bytes 24580
  6.5 65.8 %all-gather.2.cloned.1.call-start = ((), (), s32[]{:S(2)}) async-start(), calls=%async_computation | async-start | bytes 3538944 | tf_op jit(solution)/shard_map/all_gather | solution.py:85
  8.7 315.1 %all-reduce.2.cloned.1.call-start = ((), (), s32[]{:S(2)}) async-start(), calls=%async_computation.1 | async-start | bytes 12582912 | tf_op jit(solution)/shard_map/psum | solution.py:96
  10.8 64.0 %copy-start = (f32[256,2,192]{2,0,1:T(8,128)}, f32[256,2,192]{2,0,1:T(8,128)S(1)}, u32[]{:S(2)}) copy-start(f32[256,2,192]{2,0,1:T(8,128)S(1)} %copy.5) | copy-start | bytes 1179652
  106.4 2.3 copy-start.1
  106.4 2.3 copy-start.3
  114.7 1.1 copy-start.2
  115.9 6.7 %collective-permute-start = (f32[1,8,2,384]{3,0,2,1:T(1,128)S(1)}, f32[1,8,2,384]{3,0,2,1:T(1,128)S(1)}, u32[]{:S(2)}, u32[]{:S(2)}) collective-permute-start(f32[1,8,2,384]{3,0,2,1:T(1,128)S(1)} %copy.11), channel_id=1, source_target_pairs={{0,2},{2,4},{4,6},{6,8},{8,10},{10,12},{12,14},{14,0},{1,3},{3,5},... | collective-permute-start | bytes 73736 | tf_op jit(solution)/shard_map/ppermute | solution.py:14
  116.5 6.2 %collective-permute-start.1 = (f32[1,8,2,384]{3,0,2,1:T(1,128)S(1)}, f32[1,8,2,384]{3,0,2,1:T(1,128)S(1)}, u32[]{:S(2)}, u32[]{:S(2)}) collective-permute-start(f32[1,8,2,384]{3,0,2,1:T(1,128)S(1)} %copy.12), channel_id=1, source_target_pairs={{2,0},{4,2},{6,4},{8,6},{10,8},{12,10},{14,12},{0,14},{3,1},{5,3},... | collective-permute-start | bytes 73736 | tf_op jit(solution)/shard_map/ppermute | solution.py:17
  122.8 1.4 collective-permute-start.2
  122.8 1.5 collective-permute-start.3
Sparse Core Ops, SparseCore 0:
  9.5 62.7 all-gather.1
  114.8 208.9 all-reduce.1
where the time goes:
time: 334 us
  waiting for transfers between devices  261 us (78%)
  other arithmetic  32.7 us (10%)
  matrix products  14.8 us (4%)
  between operations  13.6 us (4%)
  local copies, waits for them, and re-layouts  6.04 us (2%)
  starting transfers between devices  5.44 us (2%)
    psum x1, waiting for transfers between devices, local(): summed = lax.psum(complex_times(map_rows, back, True), 'coil')  199 us
    all_gather x1, waiting for transfers between devices, local(): lax.all_gather(position_low, 'coil', axis=0, tiled=True).astype(jnp.float32)  58.9 us
    sub x1, other arithmetic, rows_apply(): out_real = real_part[..., :width] - imag_part[..., width:]  9.23 us
  transfers between devices with their start and end apart: 6, of which 6 were waited for; matrix products, arithmetic and copies ran while one was open for 1% of the time, Pallas kernels for 0%

commit v1 on v0

--- a/solution.py
+++ b/solution.py
@@ -93,7 +93,7 @@
     back_rows = rows_apply(row_real, row_imag, residual, True).astype(jnp.bfloat16)
     back = jnp.einsum("npsc,cd->npsd", back_rows, backward_wide, preferred_element_type=jnp.float32)
     map_rows = coil_map.astype(jnp.float32)[:, None]
-    summed = lax.psum(complex_times(map_rows, back, True), "coil")
+    summed = jnp.sum(lax.all_gather(complex_times(map_rows, back, True), "coil"), axis=0)
     likelihood = lax.dynamic_slice_in_dim(summed, lax.axis_index("coil") * rows_here, rows_here, 0)
     padded = with_halo(position, (("coil", 0), ("phase", 1)), 1)
     phase_part = 2.0 * position - padded[1:-1, :-2] - padded[1:-1, 2:]

time: 334 us -> 1100 us (3.29)
  waiting for transfers between devices: 261 us -> 1000 us
  other arithmetic: 32.7 us -> 52.9 us
    all_gather x0 -> x1, waiting for transfers between devices: none -> 943 us  [local(): lax.all_gather(complex_times(map_rows, back, True), 'coil')]
    psum x1 -> x0, waiting for transfers between devices: 199 us -> none  [local(): summed = lax.psum(complex_times(map_rows, back, True), 'coil')]
    reduce_sum x0 -> x1, other arithmetic: none -> 20.2 us  [local(): jnp.sum(lax.all_gather(complex_times(map_rows, back, True), 'coil'), axis=0)]
  transfers between devices with their start and end apart: 6 -> 6, of which waited for: 6 -> 4; matrix products, arithmetic and copies ran while one was open for 1% -> 2% of each run, Pallas kernels for 0% -> 0%
where the time goes in v1:
time: 1100 us
  waiting for transfers between devices  1000 us (91%)
  other arithmetic  52.9 us (5%)
  matrix products  14.8 us (1%)
  between operations  13.6 us (1%)
    all_gather x1, waiting for transfers between devices, local(): lax.all_gather(complex_times(map_rows, back, True), 'coil')  943 us
    all_gather x1, waiting for transfers between devices, local(): lax.all_gather(position_low, 'coil', axis=0, tiled=True).astype(jnp.float32)  58.9 us
  transfers between devices with their start and end apart: 6, of which 4 were waited for; matrix products, arithmetic and copies ran while one was open for 2% of the time, Pallas kernels for 0%

profile of v1, /device:TPU:0, one launch (start us, length us, event | category | flops | bytes accessed | tf_op | source)
XLA Modules:
  0.0 1096.2 jit_solution(2269197996824591500)
XLA Ops:
  6.5 0.0 copy-start.4
  6.5 0.0 all-gather.4.cloned.1.call-start
  6.5 2.1 copy.28
  8.7 0.0 all-gather.4.cloned.1.call-update
  8.7 0.0 all-gather.6.cloned.1.call-start
  8.8 1.3 bitcast_convert_fusion
  10.0 0.7 negate_bitcast_fusion
  10.8 0.0 copy-start
  10.9 0.0 copy-done.4
  10.9 0.9 copy.14
  11.8 0.8 fusion.44
  12.6 0.8 negate_convert_fusion
  13.4 58.9 %all-gather.4.cloned.1.call-done = bf16[256,8,2,384]{3,0,2,1:T(8,128)(2,1)} async-done(((bf16[32,8,2,384]{3,0,2,1:T(8,128)(2,1)}), bf16[256,8,2,384]{3,0,2,1:T(8,128)(2,1)}) %all-gather.4.cloned.1.call-update) | async-done | bytes 3145744 | tf_op jit(solution)/shard_map/all_gather | solution.py:85
  72.3 2.5 convert_element_type.81
  74.9 0.0 copy-done
  74.9 1.8 subtract_convert_fusion
  76.7 2.3 fusion.12
  79.0 1.9 fusion.49
  80.9 4.6 fusion.53
  85.4 9.2 slice_subtract_fusion.1
  94.7 5.3 fusion.1
  100.0 1.9 fusion.47
  101.9 1.9 fusion.51
  103.8 2.6 fusion.3
  106.4 0.0 copy-start.1
  106.4 0.0 copy-start.3
  106.4 2.3 fusion.8
  108.7 0.0 copy-done.1
  108.7 0.0 copy-done.3
  108.7 2.0 multiply_subtract_fusion
  110.8 3.9 pad_maximum_fusion
  114.7 0.0 copy-start.2
  114.7 0.0 all-gather.6.cloned.1.call-update
  114.7 1.1 copy-done.2
  115.9 0.6 collective-permute-start
  116.5 4.2 collective-permute-start.1
  120.7 0.3 copy.11
  121.0 1.6 collective-permute-done
  122.5 0.2 collective-permute-done.1
  122.7 0.1 collective-permute-start.2
  122.8 0.5 collective-permute-start.3
  123.3 942.7 %all-gather.6.cloned.1.call-done = f32[2048,8,2,384]{3,0,2,1:T(8,128)} async-done(((f32[256,8,2,384]{3,0,2,1:T(8,128)}), f32[2048,8,2,384]{3,0,2,1:T(8,128)}) %all-gather.6.cloned.1.call-update) | async-done | bytes 50331664 | tf_op jit(solution)/shard_map/all_gather | solution.py:96
  1066.0 20.2 %reduce_sum.9 = f32[256,8,2,384]{3,0,2,1:T(8,128)} reduce(f32[8,256,8,2,384]{4,1,0,3,2:T(8,128)} %bitcast.39, f32[]{:T(128)} %constant.45.clone.1), dimensions={0}, to_apply=%region_0.1 | reduce | flops 11010048 | bytes 56623108 | tf_op jit(solution)/shard_map/reduce_sum | solution.py:96
  1086.3 0.0 collective-permute-done.2
  1086.3 0.0 collective-permute-done.3
  1086.3 1.6 fusion.17
  1087.9 1.5 copy.21
  (7 shorter events, 0.2 us)
Async XLA Ops:
  6.5 4.3 copy-start.4
  6.5 65.8 %all-gather.4.cloned.1.call-start = ((), (), s32[]{:S(2)}) async-start(), calls=%async_computation | async-start | bytes 3538944 | tf_op jit(solution)/shard_map/all_gather | solution.py:85
  8.7 1057.3 %all-gather.6.cloned.1.call-start = ((), (), s32[]{:S(2)}) async-start(), calls=%async_computation.1 | async-start | bytes 56623104 | tf_op jit(solution)/shard_map/all_gather | solution.py:96
  10.8 64.0 %copy-start = (f32[256,2,192]{2,0,1:T(8,128)}, f32[256,2,192]{2,0,1:T(8,128)S(1)}, u32[]{:S(2)}) copy-start(f32[256,2,192]{2,0,1:T(8,128)S(1)} %copy.10) | copy-start | bytes 1179652
  106.4 2.3 copy-start.1
  106.4 2.3 copy-start.3
  114.7 1.1 copy-start.2
  115.9 6.7 collective-permute-start
  116.5 6.2 collective-permute-start.1
  122.7 963.5 %collective-permute-start.2 = (f32[34,1,2,384]{3,0,2,1:T(8,128)S(1)}, f32[34,1,2,384]{3,0,2,1:T(8,128)S(1)}, u32[]{:S(2)}, u32[]{:S(2)}) collective-permute-start(f32[34,1,2,384]{3,0,2,1:T(8,128)S(1)} %get-tuple-element.13), channel_id=1, source_target_pairs={{0,1},{1,0},{2,3},{3,2},{4,5},{5,4},{6,7},{7,6},{8,9},{9,8},{10,11... | collective-permute-start | bytes 313352 | tf_op jit(solution)/shard_map/ppermute | solution.py:14
  122.8 963.5 %collective-permute-start.3 = (f32[34,1,2,384]{3,0,2,1:T(8,128)S(1)}, f32[34,1,2,384]{3,0,2,1:T(8,128)S(1)}, u32[]{:S(2)}, u32[]{:S(2)}) collective-permute-start(f32[34,1,2,384]{3,0,2,1:T(8,128)S(1)} %get-tuple-element.14), channel_id=1, source_target_pairs={{1,0},{0,1},{3,2},{2,3},{5,4},{4,5},{7,6},{6,7},{9,8},{8,9},{11,10... | collective-permute-start | bytes 313352 | tf_op jit(solution)/shard_map/ppermute | solution.py:17
Sparse Core Ops, SparseCore 0:
  9.5 62.7 all-gather.3
  114.8 951.1 all-gather.5
